TPU v7x, 128 devices: a whole 4x4x4 slice. The times are simulated.
128 devices in a mesh: req: 16 (over x, y), mlp: 8 (over z, core).
Axes of the slice: x: 4, y: 4, z: 4, core: 2. Of those that a mesh axis runs over, the one named last changes fastest.
Arguments:
- tokens: bfloat16 [4096, 2048], P(('req', 'mlp')), may hold values from -6 to 6
- cached_states: float32 [256, 8, 256, 512], P('req', 'mlp'), may hold values from -12 to 12
- prompt_lengths: int32 [256], P('req'), may hold values from 1 to 4096, as said below
- accepted: int32 [256], P('req'), may hold values from 1 to 16, as said below
- owner_slot: int32 [256], P('req'), may hold values from 0 to 255, as said below
- w_query: bfloat16 [2048, 2048], P(None, 'mlp'), may hold values from -0.125 to 0.125
- w_key: bfloat16 [2048, 2048], P(None, 'mlp'), may hold values from -0.125 to 0.125
- w_value: bfloat16 [2048, 4096], P(None, 'mlp'), may hold values from -0.125 to 0.125
- w_gate_ret: bfloat16 [2048, 4096], P(None, 'mlp'), may hold values from -0.125 to 0.125
- w_out: bfloat16 [4096, 2048], P('mlp'), may hold values from -0.09375 to 0.09375
- w_gate: bfloat16 [2048, 4096], P('req', 'mlp'), may hold values from -0.125 to 0.125
- w_up: bfloat16 [2048, 4096], P('req', 'mlp'), may hold values from -0.125 to 0.125
- w_down: bfloat16 [4096, 2048], P('mlp', 'req'), may hold values from -0.09375 to 0.09375
Outputs:
- mixed: bfloat16 [4096, 2048], P(('req', 'mlp'))
- new_states: float32 [256, 8, 256, 512], P('req', 'mlp')
Inputs may be any that keep to these rules, and one draw needn't show every extreme that they name: `prompt_lengths`: request r belongs to tenant k = (4 r) // 256, so the four tenants hold consecutive ranges of 64 requests; its prompt length is drawn evenly from 1 to 4^(k + 3). `accepted`: number of leading drafts of request r that are kept, drawn evenly for each request. A permutation of the requests; for request r on req block i = r // 16, owner_slot[r] = j * 16 + i + c with owner block j and 0 <= c < 1, and each pair (j, c) occurs exactly once within a block.
All inputs are finite; a program needn't handle non-finite values.
Results may differ from a plain program's by a relative error of at most 0.017.
Values may be sent and summed in bfloat16 or wider, within the bound.
No kernel may reach another device: no remote copies, remote signals or barrier semaphores. Data moves between devices by JAX's collectives and lax.ppermute only.
A program may use at most 128 MiB of HBM per device.

v0:
```python
import math
import jax
import jax.numpy as jnp
from jax import lax
from jax.sharding import PartitionSpec as P

DRAFT = 16
epsilon = 1e-05


def layer_norm(inputs):
    average = jnp.mean(inputs, axis=-1, keepdims=True)
    centred = inputs - average
    variance = jnp.mean(centred * centred, axis=-1, keepdims=True)
    return centred * lax.rsqrt(variance + epsilon)


def decays(head_count, first_head):
    head_index = jnp.arange(head_count, dtype=jnp.float32) + first_head
    return 1.0 - jnp.exp2(-5.0 - head_index)


def rotate(inputs, positions):
    half_width = inputs.shape[-1] // 2
    frequencies = jnp.exp(
        -math.log(10000.0) * jnp.arange(half_width, dtype=jnp.float32) / half_width
    )
    angles = positions[:, :, None] * frequencies[None, None, :]
    cosine_part = jnp.cos(angles)[:, :, None, :]
    sine_part = jnp.sin(angles)[:, :, None, :]
    front_half = inputs[..., :half_width]
    back_half = inputs[..., half_width:]
    return jnp.concatenate(
        [
            front_half * cosine_part - back_half * sine_part,
            front_half * sine_part + back_half * cosine_part,
        ],
        axis=-1,
    )


def state_weights(states, accepted, gammas, draft_count):
    draft_pos = jnp.arange(draft_count, dtype=jnp.float32)
    accepted_f = accepted.astype(jnp.float32)
    exponent = accepted_f[:, None, None] - 1.0 - draft_pos[None, None, :]
    draft_weights = jnp.where(
        exponent >= 0, jnp.power(gammas[None, :, None], jnp.maximum(exponent, 0.0)), 0.0
    )
    old_part = jnp.power(gammas[None, :], accepted_f[:, None])[:, :, None, None] * states
    return (old_part, draft_weights)


def fold_update(key_rows, values, draft_weights):
    scaled = key_rows.astype(jnp.float32) * jnp.transpose(draft_weights, (0, 2, 1))[..., None]
    return jnp.einsum(
        "rshd,rshv->rhdv", scaled, values.astype(jnp.float32), precision=lax.Precision.HIGHEST
    )


def retain_outputs(queries, key_rows, values, states, gammas):
    draft_count = queries.shape[1]
    draft_pos = jnp.arange(draft_count, dtype=jnp.float32)
    distance = draft_pos[:, None] - draft_pos[None, :]
    decay_mask = jnp.where(
        distance[None] >= 0, jnp.power(gammas[:, None, None], jnp.maximum(distance, 0.0)[None]), 0.0
    )
    scores = jnp.einsum("rthd,rshd->rhts", queries, key_rows, preferred_element_type=jnp.float32)
    weights = (scores * decay_mask[None]).astype(jnp.bfloat16)
    within = jnp.einsum("rhts,rshv->rthv", weights, values, preferred_element_type=jnp.float32)
    carried = jnp.einsum(
        "rthd,rhdv->rthv", queries.astype(jnp.float32), states, precision=lax.Precision.HIGHEST
    )
    carried = carried * jnp.power(gammas[None, None, :, None], draft_pos[None, :, None, None] + 1.0)
    return within + carried


def per_device(
    tokens,
    cached_states,
    prompt_lengths,
    accepted,
    owner_slot,
    w_query,
    w_key,
    w_value,
    w_gate_ret,
    w_out,
    w_gate,
    w_up,
    w_down,
):
    requests = cached_states.shape[0]
    heads_here = cached_states.shape[1]
    key_width = cached_states.shape[2]
    value_width = cached_states.shape[3]
    draft_count = DRAFT
    per_peer = requests // lax.axis_size("req")
    first_head = (lax.axis_index("mlp") * heads_here).astype(jnp.float32)
    gammas = decays(heads_here, first_head)
    target_pos = owner_slot // requests * per_peer + owner_slot % per_peer
    local_ids = jnp.arange(requests, dtype=jnp.int32)
    send_order = jnp.sum(
        jnp.where(target_pos[None, :] == local_ids[:, None], local_ids[None, :], 0), axis=1
    )
    old_part, draft_weights = state_weights(cached_states, accepted, gammas, draft_count)
    group_rows = lax.all_gather(tokens, "mlp", axis=0, tiled=True)
    row_count = group_rows.shape[0]
    normed = layer_norm(group_rows.astype(jnp.float32)).astype(jnp.bfloat16)
    queries = jnp.dot(normed, w_query, preferred_element_type=jnp.float32).reshape(
        requests, draft_count, heads_here, key_width
    )
    key_rows = (
        jnp.dot(normed, w_key, preferred_element_type=jnp.float32) * (1.0 / math.sqrt(key_width))
    ).reshape(requests, draft_count, heads_here, key_width)
    values = (
        jnp.dot(normed, w_value, preferred_element_type=jnp.float32)
        .astype(jnp.bfloat16)
        .reshape(requests, draft_count, heads_here, value_width)
    )
    gate_ret = jnp.dot(normed, w_gate_ret, preferred_element_type=jnp.float32).reshape(
        requests, draft_count, heads_here, value_width
    )
    positions = (
        prompt_lengths[:, None] + jnp.arange(draft_count, dtype=jnp.int32)[None, :]
    ).astype(jnp.float32)
    rotated_q = rotate(queries, positions).astype(jnp.bfloat16)
    rotated_k = rotate(key_rows, positions).astype(jnp.bfloat16)
    fresh = old_part + fold_update(rotated_k, values, draft_weights)
    new_states = lax.all_to_all(
        jnp.take(fresh, send_order, axis=0).astype(jnp.bfloat16),
        "req",
        split_axis=0,
        concat_axis=0,
        tiled=True,
    ).astype(jnp.float32)
    outputs = retain_outputs(rotated_q, rotated_k, values, cached_states, gammas)
    joined = (
        (layer_norm(outputs) * jax.nn.silu(gate_ret))
        .astype(jnp.bfloat16)
        .reshape(row_count, heads_here * value_width)
    )
    partials = jnp.dot(joined, w_out, preferred_element_type=jnp.float32)
    share = tokens.shape[0]
    summed = lax.psum(partials.astype(jnp.bfloat16), "mlp").astype(jnp.float32)
    residual = group_rows.astype(jnp.float32) + summed
    hidden_in = layer_norm(residual).astype(jnp.bfloat16)
    residual_share = lax.dynamic_slice_in_dim(residual, lax.axis_index("mlp") * share, share, 0)
    gate_sum = jnp.dot(
        hidden_in,
        lax.all_gather(w_gate, "req", axis=0, tiled=True),
        preferred_element_type=jnp.float32,
    )
    up_sum = jnp.dot(
        hidden_in,
        lax.all_gather(w_up, "req", axis=0, tiled=True),
        preferred_element_type=jnp.float32,
    )
    hidden = (jax.nn.silu(gate_sum) * up_sum).astype(jnp.bfloat16)
    down_terms = jnp.dot(
        hidden,
        lax.all_gather(w_down, "req", axis=1, tiled=True),
        preferred_element_type=jnp.float32,
    )
    mixed = (
        residual_share
        + lax.psum_scatter(
            down_terms.astype(jnp.bfloat16), "mlp", scatter_dimension=0, tiled=True
        ).astype(jnp.float32)
    ).astype(jnp.bfloat16)
    return (mixed, new_states)


def solution(mesh):
    return jax.shard_map(
        per_device,
        mesh=mesh,
        in_specs=(
            P(("req", "mlp"), None),
            P("req", "mlp", None, None),
            P("req"),
            P("req"),
            P("req"),
            P(None, "mlp"),
            P(None, "mlp"),
            P(None, "mlp"),
            P(None, "mlp"),
            P("mlp", None),
            P("req", "mlp"),
            P("req", "mlp"),
            P("mlp", "req"),
        ),
        out_specs=(P(("req", "mlp"), None), P("req", "mlp", None, None)),
        check_vma=False,
    )
```

profile of v0, /device:TPU:0, one launch (start us, length us, event | category | flops | bytes accessed | tf_op | source)
XLA Modules:
  0.0 292.6 jit_solution(9923239641830720972)
XLA Ops:
  8.0 0.0 copy-start
  8.0 0.0 copy-start.13
  8.0 0.0 all-gather.5.cloned.1.call-start
  8.1 0.7 all-gather.5.cloned.1.call-update
  8.8 0.0 all-reduce.2.cloned.1.call-start
  8.9 1.3 convert_add_fusion.1
  10.2 0.7 add_convert_fusion.1
  10.9 0.7 power_select_fusion
  11.6 25.0 %all-gather.5.cloned.1.call-done = bf16[256,2048]{1,0:T(8,128)(2,1)} async-done(((bf16[32,2048]{1,0:T(8,128)(2,1)}), bf16[256,2048]{1,0:T(8,128)(2,1)}) %all-gather.5.cloned.1.call-update) | async-done | bytes 1048592 | tf_op jit(solution)/shard_map/all_gather | solution.py:106
  36.6 1.6 convert_reduce_fusion
  38.3 0.0 copy-start.8
  38.3 2.0 fusion.7
  40.2 0.0 copy-done.13
  40.2 0.0 copy-start.10
  40.3 1.7 fusion.62
  42.0 2.0 convolution_multiply_fusion.1
  44.0 0.6 fusion.46
  44.6 0.0 copy-start.5
  44.6 0.0 copy-start.6
  44.7 0.6 copy-done.5
  45.3 0.0 copy-done.6
  45.3 0.0 copy-done.1
  45.3 3.7 %fusion.14 = f32[16,1,512,16]{2,3,0,1:T(8,128)} fusion(f32[16,1,256,512]{3,2,1,0:T(8,128)S(1)} %copy-done.1, f32[16]{0:T(128)S(1)} %add_power_fusion, bf16[16,16,128]{2,1,0:T(8,128)(2,1)S(1)} %get-tuple-element.10, bf16[16,16,128]{2,1,0:T(8,128)(2,1)S(1)} %get-tuple-element.11), kind=kOutput, calls=%fused_computation.25 | convolution fusion | flops 403046400 | bytes 9044032 | tf_op jit(solution)/shard_map/rthd,rhdv->rthv/dot_general | solution.py:70
  49.0 0.0 copy-done.8
  49.0 0.0 copy-done.10
  49.0 0.0 copy-done.2
  49.0 0.8 convolution_convert_fusion.2
  49.7 2.2 fusion.65
  52.0 1.2 multiply_reduce_fusion.1
  53.2 0.0 copy-start.3
  53.2 2.4 fusion.59
  55.7 0.0 copy-done.3
  55.7 0.2 multiply_convert_fusion.1
  55.9 0.0 copy-start.14
  56.0 1.7 convolution_convert_fusion.1
  57.7 0.0 all-reduce.2.cloned.1.call-update
  57.7 0.0 all-gather.7.cloned.1.call-start
  57.7 0.5 all-gather.7.cloned.1.call-update
  58.3 0.0 all-gather.9.cloned.1.call-start
  58.3 0.5 all-gather.9.cloned.1.call-update
  58.9 0.0 all-gather.11.cloned.1.call-start
  58.9 0.5 all-gather.11.cloned.1.call-update
  59.5 0.1 select_reduce_fusion
  59.6 0.5 compare_and_fusion
  60.1 0.0 copy-done.7
  60.1 8.5 %fusion.1 = bf16[16,256,512]{2,1,0:T(8,128)(2,1)} fusion(f32[16,1,256,512]{3,2,1,0:T(8,128)} %param.14, f32[16]{0:T(128)S(1)} %copy-done.9, bf16[16,16,512]{2,1,0:T(8,128)(2,1)S(1)} %bitcast.68, f32[16,16]{1,0:T(8,128)S(1)} %copy-done.7, bf16[16,16,128]{2,1,0:T(8,128)(2,1)S(1)} %get-tuple-element.7, bf16[16,16,128]{2,1,0:T(8,128)(2,1)S(1)} %get-tuple-element.6), kind=kOutput, calls=%fused_computation.4 | convolution fusion | flops 409272320 | bytes 12977216 | tf_op jit(solution)/shard_map/rshd,rshv->rhdv/dot_general | solution.py:55
  68.7 5.1 %gather_fusion = bf16[16,256,512]{2,1,0:T(8,128)(2,1)} fusion(bf16[16,256,512]{2,1,0:T(8,128)(2,1)} %fusion.1, s32[1024]{0:T(1024)S(1)} %pad_clamp_fusion), kind=kCustom, calls=%fused_computation | custom fusion | bytes 8388672 | tf_op jit(solution)/shard_map/jit(_take)/gather | solution.py:130
  73.7 5.5 %fusion.4 = bf16[16,1,256,512]{3,2,1,0:T(8,128)(2,1)} fusion(bf16[16,256,512]{2,1,0:T(8,128)(2,1)} %gather_fusion, pred[16]{0:T(512)(128)(4,1)S(1)} %copy-done.11), kind=kLoop, calls=%fused_computation.8 | loop fusion | flops 2097152 | bytes 8388624 | tf_op jit(solution)/shard_map/convert_element_type | solution.py:130
  79.2 6.9 %all-to-all-start = ((bf16[16,1,256,512]{3,2,1,0:T(8,128)(2,1)}), bf16[16,1,256,512]{3,2,1,0:T(8,128)(2,1)}, u32[]{:S(2)}, u32[]{:S(2)}) async-start(bf16[16,1,256,512]{3,2,1,0:T(8,128)(2,1)} %fusion.4), calls=%async_computation.1 | async-start | bytes 8388608 | tf_op jit(solution)/shard_map/all_to_all | solution.py:129
  86.1 0.2 reduce-scatter.2.cloned.1.call-start
  86.3 35.1 %all-reduce.2.cloned.1.call-done = bf16[256,2048]{1,0:T(8,128)(2,1)} async-done(((bf16[256,2048]{1,0:T(8,128)(2,1)}), bf16[256,2048]{1,0:T(8,128)(2,1)}) %all-reduce.2.cloned.1.call-update) | async-done | bytes 1048592 | tf_op jit(solution)/shard_map/psum | solution.py:144
  121.4 2.9 convert_add_fusion
  124.3 0.0 copy-done.4
  124.3 0.5 multiply_reduce_fusion
  124.8 18.6 %all-gather.7.cloned.1.call-done = bf16[2048,512]{1,0:T(8,128)(2,1)} async-done(((bf16[128,512]{1,0:T(8,128)(2,1)}), bf16[2048,512]{1,0:T(8,128)(2,1)}) %all-gather.7.cloned.1.call-update) | async-done | bytes 2097168 | tf_op jit(solution)/shard_map/all_gather | solution.py:150
  143.5 3.5 %fusion.58 = f32[256,512]{1,0:T(8,128)} fusion(bf16[2048,512]{1,0:T(8,128)(2,1)} %all-gather.7.cloned.1.call-done, f32[256]{0:T(256)S(1)} %add_rsqrt_fusion.1, f32[256]{0:T(256)S(1)} %broadcast_multiply_fusion.1, bf16[256,2048]{1,0:T(8,128)(2,1)} %all-reduce.2.cloned.1.call-done, bf16[256,2048]{1,0:T(8,128)(2,1)S(1)} %copy-done.2), kind=kOutput, calls=%fused_computation.101 | convolution fusion | flops 540016640 | bytes 4720640 | tf_op jit(solution)/shard_map/dot_general | solution.py:148
  147.0 51.2 %all-gather.9.cloned.1.call-done = bf16[2048,512]{1,0:T(8,128)(2,1)} async-done(((bf16[128,512]{1,0:T(8,128)(2,1)}), bf16[2048,512]{1,0:T(8,128)(2,1)}) %all-gather.9.cloned.1.call-update) | async-done | bytes 2097168 | tf_op jit(solution)/shard_map/all_gather | solution.py:155
  198.2 48.6 %all-gather.11.cloned.1.call-done = bf16[512,2048]{1,0:T(8,128)(2,1)} async-done(((bf16[512,128]{1,0:T(8,128)(2,1)}), bf16[512,2048]{1,0:T(8,128)(2,1)}) %all-gather.11.cloned.1.call-update) | async-done | bytes 2097168 | tf_op jit(solution)/shard_map/all_gather | solution.py:161
  246.8 5.2 %convolution_convert_fusion = bf16[256,2048]{1,0:T(8,128)(2,1)} fusion(bf16[512,2048]{1,0:T(8,128)(2,1)} %all-gather.11.cloned.1.call-done, bf16[2048,512]{1,0:T(8,128)(2,1)} %all-gather.9.cloned.1.call-done, f32[256,512]{1,0:T(8,128)} %fusion.58, f32[256]{0:T(256)S(1)} %add_rsqrt_fusion.1, f32[256]{0:T(256)S(1)} %broadcast_multiply_fusion.1, ...), kind=kOutput, calls=%fused_computation.12 | convolution fusion | flops 1078198272 | bytes 7866368 | tf_op jit(solution)/shard_map/dot_general | solution.py:159
  252.0 0.0 reduce-scatter.2.cloned.1.call-update
  252.0 0.0 all-to-all-done
  252.0 6.7 %convert_element_type.101 = f32[16,1,256,512]{3,2,1,0:T(8,128)} convert(bf16[16,1,256,512]{3,2,1,0:T(8,128)(2,1)} %all-to-all-done) | non-fusion elementwise | flops 2097152 | bytes 12582912 | tf_op jit(solution)/shard_map/convert_element_type | solution.py:135
  258.7 24.9 %reduce-scatter.2.cloned.1.call-done = bf16[32,2048]{1,0:T(8,128)(2,1)} async-done(((bf16[256,2048]{1,0:T(8,128)(2,1)}), bf16[32,2048]{1,0:T(8,128)(2,1)}) %reduce-scatter.2.cloned.1.call-update) | async-done | bytes 131088 | tf_op jit(solution)/shard_map/reduce_scatter | solution.py:166
  283.6 1.7 add_convert_fusion
  (23 shorter events, 0.1 us)
Async XLA Ops:
  8.0 47.9 %copy-start = (bf16[512,2048]{1,0:T(8,128)(2,1)S(1)}, bf16[512,2048]{1,0:T(8,128)(2,1)}, u32[]{:S(2)}) copy-start(bf16[512,2048]{1,0:T(8,128)(2,1)} %param.22) | copy-start | bytes 6291460
  8.0 32.2 %copy-start.13 = (bf16[2048,256]{1,0:T(8,128)(2,1)S(1)}, bf16[2048,256]{1,0:T(8,128)(2,1)}, u32[]{:S(2)}) copy-start(bf16[2048,256]{1,0:T(8,128)(2,1)} %param.18) | copy-start | bytes 3145732
  8.0 28.6 %all-gather.5.cloned.1.call-start = ((), (), s32[]{:S(2)}) async-start(), calls=%async_computation.2 | async-start | bytes 1179648 | tf_op jit(solution)/shard_map/all_gather | solution.py:106
  8.8 112.6 %all-reduce.2.cloned.1.call-start = ((), (), s32[]{:S(2)}) async-start(), calls=%async_computation.3 | async-start | bytes 2097152 | tf_op jit(solution)/shard_map/psum | solution.py:144
  36.6 8.6 %copy-start.1 = (f32[16,1,256,512]{3,2,1,0:T(8,128)S(1)}, f32[16,1,256,512]{3,2,1,0:T(8,128)}, u32[]{:S(2)}) copy-start(f32[16,1,256,512]{3,2,1,0:T(8,128)} %param.14) | copy-start | bytes 25165828
  38.3 10.7 %copy-start.8 = (f32[256]{0:T(256)}, f32[256]{0:T(256)S(1)}, u32[]{:S(2)}) copy-start(f32[256]{0:T(256)S(1)} %broadcast_multiply_fusion.2) | copy-start | bytes 3076
  40.2 8.7 %copy-start.10 = (f32[256]{0:T(256)}, f32[256]{0:T(256)S(1)}, u32[]{:S(2)}) copy-start(f32[256]{0:T(256)S(1)} %add_rsqrt_fusion.2) | copy-start | bytes 3076
  44.6 0.6 copy-start.5
  44.6 0.6 copy-start.6
  45.3 3.7 %copy-start.2 = (bf16[256,2048]{1,0:T(8,128)(2,1)S(1)}, bf16[256,2048]{1,0:T(8,128)(2,1)}, u32[]{:S(2)}) copy-start(bf16[256,2048]{1,0:T(8,128)(2,1)} %all-gather.5.cloned.1.call-done) | copy-start | bytes 3145732
  45.3 3.7 %copy-start.12 = (bf16[2048,512]{1,0:T(8,128)(2,1)S(1)}, bf16[2048,512]{1,0:T(8,128)(2,1)}, u32[]{:S(2)}) copy-start(bf16[2048,512]{1,0:T(8,128)(2,1)} %param.20) | copy-start | bytes 6291460
  53.2 2.4 copy-start.3
  55.9 3.5 %copy-start.14 = (s32[16]{0:T(128)S(1)}, s32[16]{0:T(128)}, u32[]{:S(2)}) copy-start(s32[16]{0:T(128)} %param.17) | copy-start | bytes 196
  55.9 4.2 %copy-start.7 = (f32[16,16]{1,0:T(8,128)S(1)}, f32[16,16]{1,0:T(8,128)}, u32[]{:S(2)}) copy-start(f32[16,16]{1,0:T(8,128)} %get-tuple-element.16) | copy-start | bytes 3076
  55.9 4.2 %copy-start.9 = (f32[16]{0:T(128)S(1)}, f32[16]{0:T(128)}, u32[]{:S(2)}) copy-start(f32[16]{0:T(128)} %get-tuple-element.13) | copy-start | bytes 196
  57.7 85.8 %all-gather.7.cloned.1.call-start = ((), (), s32[]{:S(2)}) async-start(), calls=%async_computation.4 | async-start | bytes 2228224 | tf_op jit(solution)/shard_map/all_gather | solution.py:150
  58.3 139.9 %all-gather.9.cloned.1.call-start = ((), (), s32[]{:S(2)}) async-start(), calls=%async_computation.5 | async-start | bytes 2228224 | tf_op jit(solution)/shard_map/all_gather | solution.py:155
  58.9 187.9 %all-gather.11.cloned.1.call-start = ((), (), s32[]{:S(2)}) async-start(), calls=%async_computation.6 | async-start | bytes 2228224 | tf_op jit(solution)/shard_map/all_gather | solution.py:161
  68.7 5.1 %copy-start.11 = (pred[16]{0:T(512)(128)(4,1)S(1)}, pred[16]{0:T(512)(128)(4,1)}, u32[]{:S(2)}) copy-start(pred[16]{0:T(512)(128)(4,1)} %compare_and_fusion) | copy-start | bytes 52
  79.2 172.8 %all-to-all-start = ((bf16[16,1,256,512]{3,2,1,0:T(8,128)(2,1)}), bf16[16,1,256,512]{3,2,1,0:T(8,128)(2,1)}, u32[]{:S(2)}, u32[]{:S(2)}) async-start(bf16[16,1,256,512]{3,2,1,0:T(8,128)(2,1)} %fusion.4), calls=%async_computation.1 | async-start | bytes 8388608 | tf_op jit(solution)/shard_map/all_to_all | solution.py:129
  86.1 197.5 %reduce-scatter.2.cloned.1.call-start = ((), (), s32[]{:S(2)}) async-start(), calls=%async_computation.7 | async-start | bytes 1179648 | tf_op jit(solution)/shard_map/reduce_scatter | solution.py:166
  121.4 2.9 copy-start.4
Sparse Core Ops, SparseCore 0:
  10.6 26.0 all-gather.4
  57.8 63.5 all-reduce.1
  252.1 31.4 reduce-scatter.1
Sparse Core Ops, SparseCore 1:
  60.3 83.1 all-gather.6
  145.5 52.7 all-gather.8
  200.2 46.5 all-gather.10
where the time goes:
time: 293 us
  waiting for transfers between devices  206 us (70%)
  matrix products  31.8 us (11%)
  other arithmetic  26.4 us (9%)
  between operations  15.7 us (5%)
  starting transfers between devices  7.29 us (2%)
  local copies, waits for them, and re-layouts  5.76 us (2%)
    all_gather x1, waiting for transfers between devices, per_device(): lax.all_gather(w_up, 'req', axis=0, tiled=True)  51.2 us
    all_gather x1, waiting for transfers between devices, per_device(): lax.all_gather(w_down, 'req', axis=1, tiled=True)  48.6 us
    psum x1, waiting for transfers between devices, per_device(): summed = lax.psum(partials.astype(jnp.bfloat16), 'mlp').astype(jnp.float32)  35.1 us
    all_gather x1, waiting for transfers between devices, per_device(): group_rows = lax.all_gather(tokens, 'mlp', axis=0, tiled=True)  25 us
    reduce_scatter x1, waiting for transfers between devices, per_device(): lax.psum_scatter(down_terms.astype(jnp.bfloat16), 'mlp', scatter_dimensio...  24.9 us
    all_gather x1, waiting for transfers between devices, per_device(): lax.all_gather(w_gate, 'req', axis=0, tiled=True)  18.6 us
    dot_general x1, matrix products, fold_update(): jnp.einsum('rshd,rshv->rhdv', scaled, values.astype(jnp.float32), precisi...  8.54 us
    all_to_all x1, starting transfers between devices, per_device(): lax.all_to_all(jnp.take(fresh, send_order, axis=0).astype(jnp.bfloat16),...  6.87 us
  transfers between devices with their start and end apart: 7, of which 6 were waited for; matrix products, arithmetic and copies ran while one was open for 14% of the time, Pallas kernels for 0%

commit v1 on v0

--- a/solution.py
+++ b/solution.py
@@ -103,7 +103,12 @@
         jnp.where(target_pos[None, :] == local_ids[:, None], local_ids[None, :], 0), axis=1
     )
     old_part, draft_weights = state_weights(cached_states, accepted, gammas, draft_count)
-    group_rows = lax.all_gather(tokens, "mlp", axis=0, tiled=True)
+    ring = [tokens]
+    for hop in range(7):
+        ring.append(lax.ppermute(ring[-1], "mlp", [(dev, (dev + 1) % 8) for dev in range(8)]))
+    group_rows = jnp.roll(
+        jnp.concatenate(ring[::-1], axis=0), (lax.axis_index("mlp") + 1) * ring[0].shape[0], axis=0
+    )
     row_count = group_rows.shape[0]
     normed = layer_norm(group_rows.astype(jnp.float32)).astype(jnp.bfloat16)
     queries = jnp.dot(normed, w_query, preferred_element_type=jnp.float32).reshape(

time: 293 us -> 296 us (1.010)
  waiting for transfers between devices: 206 us -> 214 us
  matrix products: 31.8 us -> 26 us
  local copies, waits for them, and re-layouts: 5.76 us -> 10 us
  other arithmetic: 26.4 us -> 22.3 us
    ppermute x0 -> x7, waiting for transfers between devices: none -> 36.7 us  [per_device(): lax.ppermute(ring[-1], 'mlp', [(dev, (dev + 1) % 8) for dev in range(8)])]
    all_gather x1 -> x0, waiting for transfers between devices: 25 us -> none  [per_device(): group_rows = lax.all_gather(tokens, 'mlp', axis=0, tiled=True)]
    unnamed x30 -> x47, local copies, waits for them, and re-layouts: 0.7 us -> 4.9 us
    all_gather x1, waiting for transfers between devices: 51.2 us -> 47 us  [per_device(): lax.all_gather(w_up, 'req', axis=0, tiled=True)]
  transfers between devices with their start and end apart: 7 -> 13, of which waited for: 6 -> 12; matrix products, arithmetic and copies ran while one was open for 14% -> 13% of each run, Pallas kernels for 0% -> 0%
where the time goes in v1:
time: 296 us; the launch traced here: 295 us
  waiting for transfers between devices  214 us (72%)
  matrix products  26 us (9%)
  other arithmetic  22.3 us (8%)
  between operations  16.2 us (5%)
  local copies, waits for them, and re-layouts  10 us (3%)
  starting transfers between devices  7.28 us (2%)
    all_gather x1, waiting for transfers between devices, per_device(): lax.all_gather(w_down, 'req', axis=1, tiled=True)  48.6 us
    all_gather x1, waiting for transfers between devices, per_device(): lax.all_gather(w_up, 'req', axis=0, tiled=True)  47 us
    ppermute x7, waiting for transfers between devices, per_device(): lax.ppermute(ring[-1], 'mlp', [(dev, (dev + 1) % 8) for dev in range(8)])  36.7 us
    psum x1, waiting for transfers between devices, per_device(): summed = lax.psum(partials.astype(jnp.bfloat16), 'mlp').astype(jnp.float32)  34.6 us
    reduce_scatter x1, waiting for transfers between devices, per_device(): lax.psum_scatter(down_terms.astype(jnp.bfloat16), 'mlp', scatter_dimensio...  24.9 us
    all_gather x1, waiting for transfers between devices, per_device(): lax.all_gather(w_gate, 'req', axis=0, tiled=True)  20.2 us
    dot_general x1, matrix products, fold_update(): jnp.einsum('rshd,rshv->rhdv', scaled, values.astype(jnp.float32), precisi...  8.55 us
    all_to_all x1, starting transfers between devices, per_device(): lax.all_to_all(jnp.take(fresh, send_order, axis=0).astype(jnp.bfloat16),...  7.04 us
  transfers between devices with their start and end apart: 13, of which 12 were waited for; matrix products, arithmetic and copies ran while one was open for 13% of the time, Pallas kernels for 0%

profile of v1, /device:TPU:0, one launch (start us, length us, event | category | flops | bytes accessed | tf_op | source)
XLA Modules:
  0.0 295.5 jit_solution(15220082348458194882)
XLA Ops:
  8.0 0.0 copy-start
  8.0 0.0 copy-start.5
  8.0 0.0 all-reduce.2.cloned.1.call-start
  8.1 0.0 collective-permute-start
  8.1 6.4 %collective-permute-done = bf16[32,2048]{1,0:T(8,128)(2,1)S(1)} collective-permute-done((bf16[32,2048]{1,0:T(8,128)(2,1)}, bf16[32,2048]{1,0:T(8,128)(2,1)S(1)}, u32[]{:S(2)}, u32[]{:S(2)}) %collective-permute-start) | collective-permute-done | bytes 131104 | tf_op jit(solution)/shard_map/ppermute | solution.py:108
  14.5 0.0 collective-permute-start.1
  14.5 5.6 %collective-permute-done.1 = bf16[32,2048]{1,0:T(8,128)(2,1)S(1)} collective-permute-done((bf16[32,2048]{1,0:T(8,128)(2,1)S(1)}, bf16[32,2048]{1,0:T(8,128)(2,1)S(1)}, u32[]{:S(2)}, u32[]{:S(2)}) %collective-permute-start.1) | collective-permute-done | bytes 131104 | tf_op jit(solution)/shard_map/ppermute | solution.py:108
  20.1 0.0 collective-permute-start.2
  20.2 5.6 %collective-permute-done.2 = bf16[32,2048]{1,0:T(8,128)(2,1)S(1)} collective-permute-done((bf16[32,2048]{1,0:T(8,128)(2,1)S(1)}, bf16[32,2048]{1,0:T(8,128)(2,1)S(1)}, u32[]{:S(2)}, u32[]{:S(2)}) %collective-permute-start.2) | collective-permute-done | bytes 131104 | tf_op jit(solution)/shard_map/ppermute | solution.py:108
  25.7 0.0 collective-permute-start.3
  25.7 1.3 convert_add_fusion.1
  27.0 4.3 %collective-permute-done.3 = bf16[32,2048]{1,0:T(8,128)(2,1)S(1)} collective-permute-done((bf16[32,2048]{1,0:T(8,128)(2,1)S(1)}, bf16[32,2048]{1,0:T(8,128)(2,1)S(1)}, u32[]{:S(2)}, u32[]{:S(2)}) %collective-permute-start.3) | collective-permute-done | bytes 131104 | tf_op jit(solution)/shard_map/ppermute | solution.py:108
  31.3 0.7 power_select_fusion
  32.0 4.9 %collective-permute-done.4 = bf16[32,2048]{1,0:T(8,128)(2,1)S(1)} collective-permute-done((bf16[32,2048]{1,0:T(8,128)(2,1)S(1)}, bf16[32,2048]{1,0:T(8,128)(2,1)S(1)}, u32[]{:S(2)}, u32[]{:S(2)}) %collective-permute-start.4) | collective-permute-done | bytes 131104 | tf_op jit(solution)/shard_map/ppermute | solution.py:108
  36.9 0.7 add_convert_fusion.1
  37.7 4.9 %collective-permute-done.5 = bf16[32,2048]{1,0:T(8,128)(2,1)S(1)} collective-permute-done((bf16[32,2048]{1,0:T(8,128)(2,1)S(1)}, bf16[32,2048]{1,0:T(8,128)(2,1)S(1)}, u32[]{:S(2)}, u32[]{:S(2)}) %collective-permute-start.5) | collective-permute-done | bytes 131104 | tf_op jit(solution)/shard_map/ppermute | solution.py:108
  42.5 0.5 add_power_fusion
  43.1 5.1 %collective-permute-done.6 = bf16[32,2048]{1,0:T(8,128)(2,1)S(1)} collective-permute-done((bf16[32,2048]{1,0:T(8,128)(2,1)S(1)}, bf16[32,2048]{1,0:T(8,128)(2,1)S(1)}, u32[]{:S(2)}, u32[]{:S(2)}) %collective-permute-start.6) | collective-permute-done | bytes 131104 | tf_op jit(solution)/shard_map/ppermute | solution.py:108
  48.3 0.9 constant_dynamic-update-slice_fusion.8
  49.2 0.0 copy-start.11
  49.4 0.2 convert_reduce_fusion
  49.6 0.0 copy-start.12
  49.6 0.4 fusion.7
  50.0 0.7 copy-done.11
  50.7 0.5 fusion.61
  51.2 0.3 copy-done.12
  51.5 0.5 convolution_multiply_fusion.1
  52.0 1.5 copy-done.9
  53.5 0.8 convolution_convert_fusion.2
  54.3 1.6 fusion.58
  55.9 0.6 fusion.46
  56.5 0.0 copy-start.3
  56.6 2.9 fusion.14
  59.5 1.3 fusion.65
  60.8 0.2 multiply_reduce_fusion.1
  61.0 1.3 multiply_convert_fusion.1
  62.3 0.0 copy-start.13
  62.3 1.7 convolution_convert_fusion.1
  64.0 0.0 all-reduce.2.cloned.1.call-update
  64.0 0.0 all-gather.4.cloned.1.call-start
  64.1 0.5 all-gather.4.cloned.1.call-update
  64.6 0.0 all-gather.6.cloned.1.call-start
  64.7 0.5 all-gather.6.cloned.1.call-update
  65.2 0.0 all-gather.8.cloned.1.call-start
  65.2 0.5 all-gather.8.cloned.1.call-update
  65.8 0.1 select_reduce_fusion
  66.0 8.5 %fusion.1 = bf16[16,256,512]{2,1,0:T(8,128)(2,1)} fusion(f32[16,1,256,512]{3,2,1,0:T(8,128)} %param.14, f32[16]{0:T(128)S(1)} %copy-done.7, bf16[16,16,512]{2,1,0:T(8,128)(2,1)S(1)} %bitcast.70, f32[16,16]{1,0:T(8,128)S(1)} %copy-done.6, bf16[16,16,128]{2,1,0:T(8,128)(2,1)S(1)} %get-tuple-element.7, bf16[16,16,128]{2,1,0:T(8,128)(2,1)S(1)} %get-tuple-element.6), kind=kOutput, calls=%fused_computation.4 | convolution fusion | flops 409272320 | bytes 12977216 | tf_op jit(solution)/shard_map/rshd,rshv->rhdv/dot_general | solution.py:55
  74.5 5.1 %gather_fusion = bf16[16,256,512]{2,1,0:T(8,128)(2,1)} fusion(bf16[16,256,512]{2,1,0:T(8,128)(2,1)} %fusion.1, s32[1024]{0:T(1024)S(1)} %pad_clamp_fusion), kind=kCustom, calls=%fused_computation | custom fusion | bytes 8388672 | tf_op jit(solution)/shard_map/jit(_take)/gather | solution.py:135
  79.6 5.5 %fusion.4 = bf16[16,1,256,512]{3,2,1,0:T(8,128)(2,1)} fusion(bf16[16,256,512]{2,1,0:T(8,128)(2,1)} %gather_fusion, pred[16]{0:T(512)(128)(4,1)S(1)} %compare_and_fusion), kind=kLoop, calls=%fused_computation.8 | loop fusion | flops 2097152 | bytes 8388624 | tf_op jit(solution)/shard_map/convert_element_type | solution.py:135
  85.1 7.0 %all-to-all-start = ((bf16[16,1,256,512]{3,2,1,0:T(8,128)(2,1)}), bf16[16,1,256,512]{3,2,1,0:T(8,128)(2,1)}, u32[]{:S(2)}, u32[]{:S(2)}) async-start(bf16[16,1,256,512]{3,2,1,0:T(8,128)(2,1)} %fusion.4), calls=%async_computation.1 | async-start | bytes 8388608 | tf_op jit(solution)/shard_map/all_to_all | solution.py:134
  92.2 0.0 reduce-scatter.2.cloned.1.call-start
  92.2 34.6 %all-reduce.2.cloned.1.call-done = bf16[256,2048]{1,0:T(8,128)(2,1)} async-done(((bf16[256,2048]{1,0:T(8,128)(2,1)}), bf16[256,2048]{1,0:T(8,128)(2,1)}) %all-reduce.2.cloned.1.call-update) | async-done | bytes 1048592 | tf_op jit(solution)/shard_map/psum | solution.py:149
  126.8 1.9 fusion.64
  128.7 1.3 copy-done.1
  130.1 0.3 multiply_reduce_fusion
  130.4 20.2 %all-gather.4.cloned.1.call-done = bf16[2048,512]{1,0:T(8,128)(2,1)} async-done(((bf16[128,512]{1,0:T(8,128)(2,1)}), bf16[2048,512]{1,0:T(8,128)(2,1)}) %all-gather.4.cloned.1.call-update) | async-done | bytes 2097168 | tf_op jit(solution)/shard_map/all_gather | solution.py:155
  150.6 3.0 %fusion.57 = f32[256,512]{1,0:T(8,128)S(1)} fusion(bf16[2048,512]{1,0:T(8,128)(2,1)} %all-gather.4.cloned.1.call-done, f32[256,2048]{1,0:T(8,128)} %copy-done.1, f32[256]{0:T(256)S(1)} %add_rsqrt_fusion.1, f32[256]{0:T(256)S(1)} %broadcast_multiply_fusion.1), kind=kOutput, calls=%fused_computation.116 | convolution fusion | flops 538443776 | bytes 4720640 | tf_op jit(solution)/shard_map/dot_general | solution.py:153
  153.6 47.0 %all-gather.6.cloned.1.call-done = bf16[2048,512]{1,0:T(8,128)(2,1)} async-done(((bf16[128,512]{1,0:T(8,128)(2,1)}), bf16[2048,512]{1,0:T(8,128)(2,1)}) %all-gather.6.cloned.1.call-update) | async-done | bytes 2097168 | tf_op jit(solution)/shard_map/all_gather | solution.py:160
  200.6 48.6 %all-gather.8.cloned.1.call-done = bf16[512,2048]{1,0:T(8,128)(2,1)} async-done(((bf16[512,128]{1,0:T(8,128)(2,1)}), bf16[512,2048]{1,0:T(8,128)(2,1)}) %all-gather.8.cloned.1.call-update) | async-done | bytes 2097168 | tf_op jit(solution)/shard_map/all_gather | solution.py:166
  249.2 5.3 %convolution_convert_fusion = bf16[256,2048]{1,0:T(8,128)(2,1)} fusion(bf16[512,2048]{1,0:T(8,128)(2,1)} %all-gather.8.cloned.1.call-done, bf16[2048,512]{1,0:T(8,128)(2,1)} %all-gather.6.cloned.1.call-done, f32[256,512]{1,0:T(8,128)S(1)} %fusion.57, f32[256,2048]{1,0:T(8,128)} %copy-done.1, f32[256]{0:T(256)S(1)} %add_rsqrt_fusion.1, ...), kind=kOutput, calls=%fused_computation.12 | convolution fusion | flops 1076625408 | bytes 7866368 | tf_op jit(solution)/shard_map/dot_general | solution.py:164
  254.5 0.0 reduce-scatter.2.cloned.1.call-update
  254.5 6.7 %convert_element_type.101 = f32[16,1,256,512]{3,2,1,0:T(8,128)} convert(bf16[16,1,256,512]{3,2,1,0:T(8,128)(2,1)} %all-to-all-done) | non-fusion elementwise | flops 2097152 | bytes 12582912 | tf_op jit(solution)/shard_map/convert_element_type | solution.py:140
  261.2 24.9 %reduce-scatter.2.cloned.1.call-done = bf16[32,2048]{1,0:T(8,128)(2,1)} async-done(((bf16[256,2048]{1,0:T(8,128)(2,1)}), bf16[32,2048]{1,0:T(8,128)(2,1)}) %reduce-scatter.2.cloned.1.call-update) | async-done | bytes 131088 | tf_op jit(solution)/shard_map/reduce_scatter | solution.py:171
  286.2 1.7 add_convert_fusion
  (53 shorter events, 0.3 us)
Async XLA Ops:
  8.0 54.3 %copy-start = (bf16[512,2048]{1,0:T(8,128)(2,1)S(1)}, bf16[512,2048]{1,0:T(8,128)(2,1)}, u32[]{:S(2)}) copy-start(bf16[512,2048]{1,0:T(8,128)(2,1)} %param.22) | copy-start | bytes 6291460
  8.0 41.3 %copy-start.5 = (bf16[32,2048]{1,0:T(8,128)(2,1)S(1)}, bf16[32,2048]{1,0:T(8,128)(2,1)}, u32[]{:S(2)}) copy-start(bf16[32,2048]{1,0:T(8,128)(2,1)} %param.13) | copy-start | bytes 393220
  8.0 118.8 %all-reduce.2.cloned.1.call-start = ((), (), s32[]{:S(2)}) async-start(), calls=%async_computation.2 | async-start | bytes 2097152 | tf_op jit(solution)/shard_map/psum | solution.py:149
  8.1 6.4 %collective-permute-start = (bf16[32,2048]{1,0:T(8,128)(2,1)}, bf16[32,2048]{1,0:T(8,128)(2,1)S(1)}, u32[]{:S(2)}, u32[]{:S(2)}) collective-permute-start(bf16[32,2048]{1,0:T(8,128)(2,1)} %param.13), channel_id=1, source_target_pairs={{0,1},{1,2},{2,3},{3,4},{4,5},{5,6},{6,7},{7,0},{8,9},{9,10},{10,1... | collective-permute-start | bytes 393224 | tf_op jit(solution)/shard_map/ppermute | solution.py:108
  14.5 5.6 %collective-permute-start.1 = (bf16[32,2048]{1,0:T(8,128)(2,1)S(1)}, bf16[32,2048]{1,0:T(8,128)(2,1)S(1)}, u32[]{:S(2)}, u32[]{:S(2)}) collective-permute-start(bf16[32,2048]{1,0:T(8,128)(2,1)S(1)} %collective-permute-done), channel_id=1, source_target_pairs={{0,1},{1,2},{2,3},{3,4},{4,5},{5,6},{6,7},{7,0},{8,9},{9,10},{10,1... | collective-permute-start | bytes 393224 | tf_op jit(solution)/shard_map/ppermute | solution.py:108
  20.1 5.6 %collective-permute-start.2 = (bf16[32,2048]{1,0:T(8,128)(2,1)S(1)}, bf16[32,2048]{1,0:T(8,128)(2,1)S(1)}, u32[]{:S(2)}, u32[]{:S(2)}) collective-permute-start(bf16[32,2048]{1,0:T(8,128)(2,1)S(1)} %collective-permute-done.1), channel_id=1, source_target_pairs={{0,1},{1,2},{2,3},{3,4},{4,5},{5,6},{6,7},{7,0},{8,9},{9,10},{10,1... | collective-permute-start | bytes 393224 | tf_op jit(solution)/shard_map/ppermute | solution.py:108
  25.7 5.6 %collective-permute-start.3 = (bf16[32,2048]{1,0:T(8,128)(2,1)S(1)}, bf16[32,2048]{1,0:T(8,128)(2,1)S(1)}, u32[]{:S(2)}, u32[]{:S(2)}) collective-permute-start(bf16[32,2048]{1,0:T(8,128)(2,1)S(1)} %collective-permute-done.2), channel_id=1, source_target_pairs={{0,1},{1,2},{2,3},{3,4},{4,5},{5,6},{6,7},{7,0},{8,9},{9,10},{10,1... | collective-permute-start | bytes 393224 | tf_op jit(solution)/shard_map/ppermute | solution.py:108
  31.3 5.6 %collective-permute-start.4 = (bf16[32,2048]{1,0:T(8,128)(2,1)S(1)}, bf16[32,2048]{1,0:T(8,128)(2,1)S(1)}, u32[]{:S(2)}, u32[]{:S(2)}) collective-permute-start(bf16[32,2048]{1,0:T(8,128)(2,1)S(1)} %collective-permute-done.3), channel_id=1, source_target_pairs={{0,1},{1,2},{2,3},{3,4},{4,5},{5,6},{6,7},{7,0},{8,9},{9,10},{10,1... | collective-permute-start | bytes 393224 | tf_op jit(solution)/shard_map/ppermute | solution.py:108
  36.9 5.6 %collective-permute-start.5 = (bf16[32,2048]{1,0:T(8,128)(2,1)S(1)}, bf16[32,2048]{1,0:T(8,128)(2,1)S(1)}, u32[]{:S(2)}, u32[]{:S(2)}) collective-permute-start(bf16[32,2048]{1,0:T(8,128)(2,1)S(1)} %collective-permute-done.4), channel_id=1, source_target_pairs={{0,1},{1,2},{2,3},{3,4},{4,5},{5,6},{6,7},{7,0},{8,9},{9,10},{10,1... | collective-permute-start | bytes 393224 | tf_op jit(solution)/shard_map/ppermute | solution.py:108
  42.5 5.6 %collective-permute-start.6 = (bf16[32,2048]{1,0:T(8,128)(2,1)S(1)}, bf16[32,2048]{1,0:T(8,128)(2,1)S(1)}, u32[]{:S(2)}, u32[]{:S(2)}) collective-permute-start(bf16[32,2048]{1,0:T(8,128)(2,1)S(1)} %collective-permute-done.5), channel_id=1, source_target_pairs={{0,1},{1,2},{2,3},{3,4},{4,5},{5,6},{6,7},{7,0},{8,9},{9,10},{10,1... | collective-permute-start | bytes 393224 | tf_op jit(solution)/shard_map/ppermute | solution.py:108
  49.2 1.5 copy-start.11
  49.4 5.0 %copy-start.2 = (bf16[512,2048]{1,0:T(8,128)(2,1)}, bf16[512,2048]{1,0:T(8,128)(2,1)S(1)}, u32[]{:S(2)}) copy-start(bf16[512,2048]{1,0:T(8,128)(2,1)S(1)} %constant_dynamic-update-slice_fusion) | copy-start | bytes 6291460
  49.6 1.9 copy-start.12
  50.7 5.8 %slice-start = ((s8[8388608]{0:T(1024)(128)(4,1)}), s8[4194304]{0:T(1024)(128)(4,1)S(1)}, s32[]{:S(2)}) async-start(s8[8388608]{0:T(1024)(128)(4,1)} %bitcast.67), calls=%async_computation.7 | async-start | bytes 8388608
  51.5 2.0 copy-start.9
  51.5 2.8 copy-start.10
  53.5 3.1 %slice-start.1 = ((s8[8388608]{0:T(1024)(128)(4,1)}), s8[4194304]{0:T(1024)(128)(4,1)S(1)}, s32[]{:S(2)}) async-start(s8[8388608]{0:T(1024)(128)(4,1)} %bitcast.67), calls=%async_computation.8 | async-start | bytes 8388608
  54.3 2.3 copy-start.8
  56.5 2.9 copy-start.3
  56.5 2.9 copy-start.4
  62.3 3.5 %copy-start.13 = (s32[16]{0:T(128)S(1)}, s32[16]{0:T(128)}, u32[]{:S(2)}) copy-start(s32[16]{0:T(128)} %param.17) | copy-start | bytes 196
  62.3 3.7 %copy-start.6 = (f32[16,16]{1,0:T(8,128)S(1)}, f32[16,16]{1,0:T(8,128)}, u32[]{:S(2)}) copy-start(f32[16,16]{1,0:T(8,128)} %get-tuple-element.16) | copy-start | bytes 3076
  62.3 3.7 %copy-start.7 = (f32[16]{0:T(128)S(1)}, f32[16]{0:T(128)}, u32[]{:S(2)}) copy-start(f32[16]{0:T(128)} %get-tuple-element.13) | copy-start | bytes 196
  64.0 86.6 %all-gather.4.cloned.1.call-start = ((), (), s32[]{:S(2)}) async-start(), calls=%async_computation.3 | async-start | bytes 2228224 | tf_op jit(solution)/shard_map/all_gather | solution.py:155
  64.6 136.0 %all-gather.6.cloned.1.call-start = ((), (), s32[]{:S(2)}) async-start(), calls=%async_computation.4 | async-start | bytes 2228224 | tf_op jit(solution)/shard_map/all_gather | solution.py:160
  65.2 184.0 %all-gather.8.cloned.1.call-start = ((), (), s32[]{:S(2)}) async-start(), calls=%async_computation.5 | async-start | bytes 2228224 | tf_op jit(solution)/shard_map/all_gather | solution.py:166
  85.1 169.4 %all-to-all-start = ((bf16[16,1,256,512]{3,2,1,0:T(8,128)(2,1)}), bf16[16,1,256,512]{3,2,1,0:T(8,128)(2,1)}, u32[]{:S(2)}, u32[]{:S(2)}) async-start(bf16[16,1,256,512]{3,2,1,0:T(8,128)(2,1)} %fusion.4), calls=%async_computation.1 | async-start | bytes 8388608 | tf_op jit(solution)/shard_map/all_to_all | solution.py:134
  92.2 194.0 %reduce-scatter.2.cloned.1.call-start = ((), (), s32[]{:S(2)}) async-start(), calls=%async_computation.6 | async-start | bytes 1179648 | tf_op jit(solution)/shard_map/reduce_scatter | solution.py:171
  128.7 1.4 copy-start.1
Sparse Core Ops, SparseCore 0:
  64.1 62.6 all-reduce.1
  254.6 31.5 reduce-scatter.1
Sparse Core Ops, SparseCore 1:
  66.6 83.9 all-gather.3
  152.6 48.0 all-gather.5
  202.6 46.5 all-gather.7
